TPU v7x, 32 devices: a whole 2x2x4 slice. The times are simulated.
32 devices in a mesh: groups: 2 (over y), expert: 4 (over z), dp: 4 (over x, core).
Axes of the slice: x: 2, y: 2, z: 4, core: 2. Of those that a mesh axis runs over, the one named last changes fastest.
Arguments:
- tokens: bfloat16 [4096, 2048], P(('groups', 'expert', 'dp')), parts along dimension 0, may hold values from -6 to 6
- cotangent: bfloat16 [4096, 2048], P(('groups', 'expert', 'dp')), parts along dimension 0, may hold values from -1.5 to 1.5
- expert_ids: int32 [4096, 8], P(('groups', 'expert', 'dp')), parts along dimension 0, may hold values from 0 to 127, all different within a row; in each aligned block of 128 rows (0 to 127, 128 to 255, ...) at most 16 rows name the same one
- gate_probs: float32 [4096, 8], P(('groups', 'expert', 'dp')), parts along dimension 0, may hold values from 0.05 to 0.6
- w_gate: bfloat16 [4, 2048, 384], P('expert', 'dp'), may hold values from -0.125 to 0.125
- w_up: bfloat16 [4, 2048, 384], P('expert', 'dp'), may hold values from -0.125 to 0.125
- w_down: bfloat16 [4, 384, 2048], P('expert', None, 'dp'), may hold values from -0.3125 to 0.3125
Outputs:
- mixed: bfloat16 [4096, 2048], P(('groups', 'expert', 'dp')), parts along dimension 0
- grad_tokens: bfloat16 [4096, 2048], P(('groups', 'expert', 'dp')), parts along dimension 0
- grad_gates: float32 [4096, 8], P(('groups', 'expert', 'dp')), parts along dimension 0
- grad_w_gate: bfloat16 [8, 2048, 384], P(('groups', 'expert'), 'dp'), parts along dimension 0
- grad_w_up: bfloat16 [8, 2048, 384], P(('groups', 'expert'), 'dp'), parts along dimension 0
- grad_w_down: bfloat16 [8, 384, 2048], P(('groups', 'expert'), None, 'dp'), parts along dimension 0
There are 2 independent parts, one for each index of `groups`. A program takes and returns all parts, laid end to end along the dimension named above; an argument that names none is the same for every part. Nothing has to cross between parts.
Inputs may be any that keep to these rules, and one draw needn't show every extreme that they name: `expert_ids`: each token names 8 different experts. In the rows of one device (aligned blocks of 128 tokens) no expert is named more than 16 times, and in every draw some expert is named exactly 16 times in some block.
All inputs are finite; a program needn't handle non-finite values.
Results may differ from a plain program's by a relative error of at most 0.0058.
Values may be sent and summed in bfloat16 or wider, within the bound.
No kernel may reach another device: no remote copies, remote signals or barrier semaphores. Data moves between devices by JAX's collectives and lax.ppermute only.
A program may use at most 128 MiB of HBM per device.

v0:
```python
import jax
import jax.numpy as jnp
from jax import lax
from jax.sharding import PartitionSpec as P

EXPERTS = 128


def dot_last(left, right):
    return lax.dot_general(
        left, right, (((1,), (1,)), ((), ())), preferred_element_type=jnp.float32
    )


def expert_rows(rows_x, rows_dy, gate_full, up_full, down_full):
    gate_part = jnp.dot(rows_x, gate_full, preferred_element_type=jnp.float32)
    up_part = jnp.dot(rows_x, up_full, preferred_element_type=jnp.float32)
    sigmoid_gate = jax.nn.sigmoid(gate_part)
    activated = gate_part * sigmoid_gate
    hidden = (activated * up_part).astype(jnp.bfloat16)
    expert_out = jnp.dot(hidden, down_full, preferred_element_type=jnp.float32).astype(jnp.bfloat16)
    back_hidden = dot_last(rows_dy, down_full)
    d_gate = (
        back_hidden * up_part * sigmoid_gate * (1.0 + gate_part * (1.0 - sigmoid_gate))
    ).astype(jnp.bfloat16)
    d_up = (back_hidden * activated).astype(jnp.bfloat16)
    d_rows = (dot_last(d_gate, gate_full) + dot_last(d_up, up_full)).astype(jnp.bfloat16)
    return (hidden, expert_out, d_gate, d_up, d_rows)


def on_device(tokens, cotangent, expert_ids, gate_probs, w_gate, w_up, w_down):
    expert_count = lax.axis_size("expert")
    dp_count = lax.axis_size("dp")
    token_rows, model_width = tokens.shape
    top_count = expert_ids.shape[1]
    slice_width = w_gate.shape[1]
    hidden_width = w_gate.shape[2]
    capacity = 2 * token_rows * top_count // EXPERTS
    slot_total = expert_count * capacity
    flat_ids = expert_ids.reshape(-1)
    onehot = (flat_ids[:, None] == jnp.arange(EXPERTS, dtype=jnp.int32)[None, :]).astype(jnp.int32)
    running = jnp.cumsum(onehot, axis=0)
    slot_index = jnp.sum(running * onehot, axis=1) - 1
    in_wave = flat_ids < expert_count
    position = jnp.where(in_wave, flat_ids * capacity + slot_index, slot_total)
    matched = position[:, None] == jnp.arange(slot_total, dtype=jnp.int32)[None, :]
    owner_row = jnp.arange(token_rows * top_count, dtype=jnp.int32) // top_count
    source = jnp.sum(jnp.where(matched, owner_row[:, None], 0), axis=0)
    filled = jnp.any(matched, axis=0)
    zero_value = jnp.zeros((), jnp.bfloat16)
    send_x = jnp.where(filled[:, None], jnp.take(tokens, source, axis=0), zero_value).reshape(
        expert_count, capacity, model_width
    )
    send_dy = jnp.where(filled[:, None], jnp.take(cotangent, source, axis=0), zero_value).reshape(
        expert_count, capacity, model_width
    )
    gate_full, up_full, down_full = (
        lax.all_gather(w_gate, "dp", axis=1, tiled=True),
        lax.all_gather(w_up, "dp", axis=1, tiled=True),
        lax.all_gather(w_down, "dp", axis=2, tiled=True),
    )
    gate_full = gate_full[0]
    up_full = up_full[0]
    down_full = down_full[0]
    got_x, got_dy = (
        lax.all_to_all(send_x, "expert", split_axis=0, concat_axis=0, tiled=True),
        lax.all_to_all(send_dy, "expert", split_axis=0, concat_axis=0, tiled=True),
    )
    rows_x = got_x.reshape(slot_total, model_width)
    rows_dy = got_dy.reshape(slot_total, model_width)
    hidden, expert_out, d_gate, d_up, d_rows = expert_rows(
        rows_x, rows_dy, gate_full, up_full, down_full
    )
    back_out, back_rows = (
        lax.all_to_all(
            expert_out.reshape(expert_count, capacity, model_width),
            "expert",
            split_axis=0,
            concat_axis=0,
            tiled=True,
        ),
        lax.all_to_all(
            d_rows.reshape(expert_count, capacity, model_width),
            "expert",
            split_axis=0,
            concat_axis=0,
            tiled=True,
        ),
    )
    back_out = back_out.reshape(slot_total, model_width)
    back_rows = back_rows.reshape(slot_total, model_width)
    matched_three = matched.reshape(token_rows, top_count, slot_total)
    weight_table = jnp.sum(jnp.where(matched_three, gate_probs[:, :, None], 0.0), axis=1)
    mixed = jnp.dot(
        weight_table, back_out.astype(jnp.float32), precision=lax.Precision.HIGHEST
    ).astype(jnp.bfloat16)
    grad_tokens = jnp.dot(
        weight_table, back_rows.astype(jnp.float32), precision=lax.Precision.HIGHEST
    ).astype(jnp.bfloat16)
    inner_table = dot_last(cotangent, back_out)
    grad_gates = jnp.sum(jnp.where(matched_three, inner_table[:, None, :], 0.0), axis=2)
    local_gate = jnp.einsum("sd,sf->df", rows_x, d_gate, preferred_element_type=jnp.float32).astype(
        jnp.bfloat16
    )
    local_up = jnp.einsum("sd,sf->df", rows_x, d_up, preferred_element_type=jnp.float32).astype(
        jnp.bfloat16
    )
    local_down = jnp.einsum(
        "sd,sf->df", rows_dy, hidden, preferred_element_type=jnp.float32
    ).astype(jnp.bfloat16)
    got_gate, got_up, got_down = (
        lax.all_to_all(
            local_gate.reshape(dp_count, slice_width, hidden_width),
            "dp",
            split_axis=0,
            concat_axis=0,
            tiled=True,
        ),
        lax.all_to_all(
            local_up.reshape(dp_count, slice_width, hidden_width),
            "dp",
            split_axis=0,
            concat_axis=0,
            tiled=True,
        ),
        lax.all_to_all(
            local_down.reshape(dp_count, slice_width, hidden_width),
            "dp",
            split_axis=0,
            concat_axis=0,
            tiled=True,
        ),
    )
    grad_w_gate = jnp.sum(got_gate.astype(jnp.float32), axis=0).astype(jnp.bfloat16)[None]
    grad_w_up = jnp.sum(got_up.astype(jnp.float32), axis=0).astype(jnp.bfloat16)[None]
    grad_w_down = jnp.sum(got_down.astype(jnp.float32), axis=0).T.astype(jnp.bfloat16)[None]
    return (mixed, grad_tokens, grad_gates, grad_w_gate, grad_w_up, grad_w_down)


def solution(mesh):
    in_specs = (
        P(("groups", "expert", "dp"), None),
        P(("groups", "expert", "dp"), None),
        P(("groups", "expert", "dp"), None),
        P(("groups", "expert", "dp"), None),
        P("expert", "dp", None),
        P("expert", "dp", None),
        P("expert", None, "dp"),
    )
    out_specs = (
        P(("groups", "expert", "dp"), None),
        P(("groups", "expert", "dp"), None),
        P(("groups", "expert", "dp"), None),
        P(("groups", "expert"), "dp", None),
        P(("groups", "expert"), "dp", None),
        P(("groups", "expert"), None, "dp"),
    )
    return jax.shard_map(
        on_device, mesh=mesh, in_specs=in_specs, out_specs=out_specs, check_vma=False
    )
```

profile of v0, /device:TPU:0, one launch (start us, length us, event | category | flops | bytes accessed | tf_op | source)
XLA Modules:
  0.0 183.9 jit_solution(1787334633764432873)
XLA Ops:
  13.9 15.0 %all_to_all.35 = bf16[4,16,2048]{2,1,0:T(8,128)(2,1)S(1)} all-to-all(bf16[4,16,2048]{2,1,0:T(8,128)(2,1)S(1)} %bitcast.74), channel_id=1, replica_groups=mesh['groups'=2,'expert'=4,'dp'=4] {'expert'}, dimensions={0} | all-to-all | bytes 524288 | tf_op jit(solution)/shard_map/all_to_all | solution.py:66
  28.9 3.4 %all-to-all-start.2 = ((bf16[4,16,2048]{2,1,0:T(8,128)(2,1)}), bf16[4,16,2048]{2,1,0:T(8,128)(2,1)S(1)}, u32[]{:S(2)}, u32[]{:S(2)}) async-start(bf16[4,16,2048]{2,1,0:T(8,128)(2,1)} %bitcast.10), calls=%async_computation.2 | async-start | bytes 524288 | tf_op jit(solution)/shard_map/all_to_all | solution.py:67
  32.3 1.8 fusion.9
  34.1 19.1 %all-gather.6.cloned.1.call-done = bf16[1,2048,384]{2,1,0:T(8,128)(2,1)} async-done(((bf16[1,512,384]{2,1,0:T(8,128)(2,1)}), bf16[1,2048,384]{2,1,0:T(8,128)(2,1)}) %all-gather.6.cloned.1.call-update) | async-done | bytes 1572880 | tf_op jit(solution)/shard_map/all_gather | solution.py:59
  53.2 1.8 fusion.5
  55.0 19.5 %all-gather.8.cloned.1.call-done = bf16[1,384,2048]{2,1,0:T(8,128)(2,1)} async-done(((bf16[1,384,512]{2,1,0:T(8,128)(2,1)}), bf16[1,384,2048]{2,1,0:T(8,128)(2,1)}) %all-gather.8.cloned.1.call-update) | async-done | bytes 1572880 | tf_op jit(solution)/shard_map/all_gather | solution.py:60
  74.5 2.1 %multiply_convert_fusion = (bf16[64,384]{1,0:T(8,128)(2,1)S(1)}, bf16[64,384]{1,0:T(8,128)(2,1)S(1)}, bf16[64,384]{1,0:T(8,128)(2,1)S(1)}) fusion(f32[64,384]{1,0:T(8,128)S(1)} %fusion.9, f32[64,384]{1,0:T(8,128)S(1)} %fusion.5, bf16[64,2048]{1,0:T(8,128)(2,1)S(1)} %bitcast.70, bf16[1,384,2048]{2,1,0:T(8,128)(2,1)} %all-gather.8.cloned.1.call-done), kind=kOutput, calls=%fused_computation.37 | convolution fusion | flops 101031936 | bytes 2179072 | tf_op jit(solution)/shard_map/dot_general | solution.py:10
  77.7 4.7 %all-to-all-start.1 = ((bf16[4,16,2048]{2,1,0:T(8,128)(2,1)}), bf16[4,16,2048]{2,1,0:T(8,128)(2,1)S(1)}, u32[]{:S(2)}, u32[]{:S(2)}) async-start(bf16[4,16,2048]{2,1,0:T(8,128)(2,1)} %bitcast.8), calls=%async_computation.1 | async-start | bytes 524288 | tf_op jit(solution)/shard_map/all_to_all | solution.py:75
  82.5 2.0 %fusion.7 = f32[64,2048]{1,0:T(8,128)S(1)} fusion(bf16[64,384]{1,0:T(8,128)(2,1)S(1)} %get-tuple-element.28, bf16[1,2048,384]{2,1,0:T(8,128)(2,1)} %all-gather.4.cloned.1.call-done), kind=kOutput, calls=%fused_computation.16 | convolution fusion | flops 100663296 | bytes 2146304 | tf_op jit(solution)/shard_map/dot_general | solution.py:10
  85.8 6.0 %all-to-all-done.1 = bf16[4,16,2048]{2,1,0:T(8,128)(2,1)S(1)} async-done(((bf16[4,16,2048]{2,1,0:T(8,128)(2,1)}), bf16[4,16,2048]{2,1,0:T(8,128)(2,1)S(1)}, u32[]{:S(2)}, u32[]{:S(2)}) %all-to-all-start.1) | async-done | bytes 262176 | tf_op jit(solution)/shard_map/all_to_all | solution.py:75
  91.8 3.4 %all-to-all-start.3 = ((bf16[4,16,2048]{2,1,0:T(8,128)(2,1)}), bf16[4,16,2048]{2,1,0:T(8,128)(2,1)S(1)}, u32[]{:S(2)}, u32[]{:S(2)}) async-start(bf16[4,16,2048]{2,1,0:T(8,128)(2,1)} %bitcast.12), calls=%async_computation.3 | async-start | bytes 524288 | tf_op jit(solution)/shard_map/all_to_all | solution.py:82
  95.2 1.8 convolution_convert_fusion.2
  97.0 5.1 %all-to-all-done.3 = bf16[4,16,2048]{2,1,0:T(8,128)(2,1)S(1)} async-done(((bf16[4,16,2048]{2,1,0:T(8,128)(2,1)}), bf16[4,16,2048]{2,1,0:T(8,128)(2,1)S(1)}, u32[]{:S(2)}, u32[]{:S(2)}) %all-to-all-start.3) | async-done | bytes 262176 | tf_op jit(solution)/shard_map/all_to_all | solution.py:82
  102.1 3.6 %all-to-all-start.4 = ((bf16[4,512,384]{2,1,0:T(8,128)(2,1)}), bf16[4,512,384]{2,1,0:T(8,128)(2,1)S(1)}, u32[]{:S(2)}, u32[]{:S(2)}) async-start(bf16[4,512,384]{2,1,0:T(8,128)(2,1)} %bitcast.67), calls=%async_computation.4 | async-start | bytes 3145728 | tf_op jit(solution)/shard_map/all_to_all | solution.py:112
  105.7 1.8 convolution_convert_fusion
  107.4 18.3 %all-to-all-done.4 = bf16[4,512,384]{2,1,0:T(8,128)(2,1)S(1)} async-done(((bf16[4,512,384]{2,1,0:T(8,128)(2,1)}), bf16[4,512,384]{2,1,0:T(8,128)(2,1)S(1)}, u32[]{:S(2)}, u32[]{:S(2)}) %all-to-all-start.4) | async-done | bytes 1572896 | tf_op jit(solution)/shard_map/all_to_all | solution.py:112
  125.7 4.3 %all-to-all-start.6 = ((bf16[4,512,384]{2,1,0:T(8,128)(2,1)}), bf16[4,512,384]{2,1,0:T(8,128)(2,1)}, u32[]{:S(2)}, u32[]{:S(2)}) async-start(bf16[4,512,384]{2,1,0:T(8,128)(2,1)} %bitcast.66), calls=%async_computation.6 | async-start | bytes 3145728 | tf_op jit(solution)/shard_map/all_to_all | solution.py:126
  130.1 1.8 convolution_convert_fusion.1
  131.8 18.4 %all-to-all-done.6 = bf16[4,512,384]{2,1,0:T(8,128)(2,1)} async-done(((bf16[4,512,384]{2,1,0:T(8,128)(2,1)}), bf16[4,512,384]{2,1,0:T(8,128)(2,1)}, u32[]{:S(2)}, u32[]{:S(2)}) %all-to-all-start.6) | async-done | bytes 1572896 | tf_op jit(solution)/shard_map/all_to_all | solution.py:126
  150.2 4.5 %all-to-all-start.5 = ((bf16[4,512,384]{2,1,0:T(8,128)(2,1)}), bf16[4,512,384]{2,1,0:T(8,128)(2,1)}, u32[]{:S(2)}, u32[]{:S(2)}) async-start(bf16[4,512,384]{2,1,0:T(8,128)(2,1)} %bitcast.65), calls=%async_computation.5 | async-start | bytes 3145728 | tf_op jit(solution)/shard_map/all_to_all | solution.py:119
  157.2 1.4 convolution_convert_fusion.3
  158.7 1.8 reduce_sum.78
  162.5 12.4 %all-to-all-done.5 = bf16[4,512,384]{2,1,0:T(8,128)(2,1)} async-done(((bf16[4,512,384]{2,1,0:T(8,128)(2,1)}), bf16[4,512,384]{2,1,0:T(8,128)(2,1)}, u32[]{:S(2)}, u32[]{:S(2)}) %all-to-all-start.5) | async-done | bytes 1572896 | tf_op jit(solution)/shard_map/all_to_all | solution.py:119
  174.8 2.5 %reduce_sum.77 = bf16[512,384]{1,0:T(8,128)(2,1)} reduce(bf16[4,512,384]{2,1,0:T(8,128)(2,1)} %all-to-all-done.5, bf16[]{:T(256)} %constant.50.clone.1), dimensions={0}, to_apply=%region_8.10 | reduce | flops 589824 | bytes 1966082 | tf_op jit(solution)/shard_map/reduce_sum | solution.py:135
  (50 shorter events, 13.6 us)
Async XLA Ops:
  7.2 4.3 %copy-start = (bf16[128,2048]{1,0:T(8,128)(2,1)S(1)}, bf16[128,2048]{1,0:T(8,128)(2,1)}, u32[]{:S(2)}) copy-start(bf16[128,2048]{1,0:T(8,128)(2,1)} %param.10) | copy-start | bytes 1572868
  7.2 25.2 %all-gather.4.cloned.1.call-start = ((), (), s32[]{:S(2)}) async-start(), calls=%async_computation.7 | async-start | bytes 1966080 | tf_op jit(solution)/shard_map/all_gather | solution.py:58
  7.9 45.3 %all-gather.6.cloned.1.call-start = ((), (), s32[]{:S(2)}) async-start(), calls=%async_computation.8 | async-start | bytes 1966080 | tf_op jit(solution)/shard_map/all_gather | solution.py:59
  8.7 65.8 %all-gather.8.cloned.1.call-start = ((), (), s32[]{:S(2)}) async-start(), calls=%async_computation.9 | async-start | bytes 1966080 | tf_op jit(solution)/shard_map/all_gather | solution.py:60
  10.9 1.3 copy-start.1
  28.9 26.1 %all-to-all-start.2 = ((bf16[4,16,2048]{2,1,0:T(8,128)(2,1)}), bf16[4,16,2048]{2,1,0:T(8,128)(2,1)S(1)}, u32[]{:S(2)}, u32[]{:S(2)}) async-start(bf16[4,16,2048]{2,1,0:T(8,128)(2,1)} %bitcast.10), calls=%async_computation.2 | async-start | bytes 524288 | tf_op jit(solution)/shard_map/all_to_all | solution.py:67
  74.5 2.1 %copy-start.2 = (bf16[1,384,2048]{2,1,0:T(8,128)(2,1)S(1)}, bf16[1,384,2048]{2,1,0:T(8,128)(2,1)}, u32[]{:S(2)}) copy-start(bf16[1,384,2048]{2,1,0:T(8,128)(2,1)} %all-gather.8.cloned.1.call-done) | copy-start | bytes 4718596
  77.7 6.7 %copy-start.3 = (bf16[1,2048,384]{2,1,0:T(8,128)(2,1)S(1)}, bf16[1,2048,384]{2,1,0:T(8,128)(2,1)}, u32[]{:S(2)}) copy-start(bf16[1,2048,384]{2,1,0:T(8,128)(2,1)} %all-gather.6.cloned.1.call-done) | copy-start | bytes 4718596
  77.7 14.0 %all-to-all-start.1 = ((bf16[4,16,2048]{2,1,0:T(8,128)(2,1)}), bf16[4,16,2048]{2,1,0:T(8,128)(2,1)S(1)}, u32[]{:S(2)}, u32[]{:S(2)}) async-start(bf16[4,16,2048]{2,1,0:T(8,128)(2,1)} %bitcast.8), calls=%async_computation.1 | async-start | bytes 524288 | tf_op jit(solution)/shard_map/all_to_all | solution.py:75
  91.8 10.3 %all-to-all-start.3 = ((bf16[4,16,2048]{2,1,0:T(8,128)(2,1)}), bf16[4,16,2048]{2,1,0:T(8,128)(2,1)S(1)}, u32[]{:S(2)}, u32[]{:S(2)}) async-start(bf16[4,16,2048]{2,1,0:T(8,128)(2,1)} %bitcast.12), calls=%async_computation.3 | async-start | bytes 524288 | tf_op jit(solution)/shard_map/all_to_all | solution.py:82
  102.1 23.6 %all-to-all-start.4 = ((bf16[4,512,384]{2,1,0:T(8,128)(2,1)}), bf16[4,512,384]{2,1,0:T(8,128)(2,1)S(1)}, u32[]{:S(2)}, u32[]{:S(2)}) async-start(bf16[4,512,384]{2,1,0:T(8,128)(2,1)} %bitcast.67), calls=%async_computation.4 | async-start | bytes 3145728 | tf_op jit(solution)/shard_map/all_to_all | solution.py:112
  125.7 24.5 %all-to-all-start.6 = ((bf16[4,512,384]{2,1,0:T(8,128)(2,1)}), bf16[4,512,384]{2,1,0:T(8,128)(2,1)}, u32[]{:S(2)}, u32[]{:S(2)}) async-start(bf16[4,512,384]{2,1,0:T(8,128)(2,1)} %bitcast.66), calls=%async_computation.6 | async-start | bytes 3145728 | tf_op jit(solution)/shard_map/all_to_all | solution.py:126
  150.2 4.6 %copy-start.4 = (s32[128,8]{0,1:T(8,128)S(1)}, s32[128,8]{0,1:T(8,128)}, u32[]{:S(2)}) copy-start(s32[128,8]{0,1:T(8,128)} %param.11) | copy-start | bytes 12292
  150.2 5.0 %copy-start.5 = (f32[128,8]{0,1:T(8,128)S(1)}, f32[128,8]{0,1:T(8,128)}, u32[]{:S(2)}) copy-start(f32[128,8]{0,1:T(8,128)} %param.12) | copy-start | bytes 12292
  150.2 24.6 %all-to-all-start.5 = ((bf16[4,512,384]{2,1,0:T(8,128)(2,1)}), bf16[4,512,384]{2,1,0:T(8,128)(2,1)}, u32[]{:S(2)}, u32[]{:S(2)}) async-start(bf16[4,512,384]{2,1,0:T(8,128)(2,1)} %bitcast.65), calls=%async_computation.5 | async-start | bytes 3145728 | tf_op jit(solution)/shard_map/all_to_all | solution.py:119
Sparse Core Ops, SparseCore 0:
  9.6 22.3 all-gather.3
  33.5 19.6 all-gather.5
  54.8 19.6 all-gather.7
where the time goes:
time: 185 us; the launch traced here: 184 us
  waiting for transfers between devices  101 us (55%)
  starting transfers between devices  24 us (13%)
  matrix products  18.5 us (10%)
  blocking collectives  15 us (8%)
  between operations  14 us (8%)
  other arithmetic  7.8 us (4%)
  local copies, waits for them, and re-layouts  3.77 us (2%)
    all_gather x1, waiting for transfers between devices, on_device(): lax.all_gather(w_down, 'dp', axis=2, tiled=True)  19.5 us
    all_gather x1, waiting for transfers between devices, on_device(): lax.all_gather(w_up, 'dp', axis=1, tiled=True)  19.1 us
    all_to_all x1, waiting for transfers between devices, on_device(): lax.all_to_all(local_down.reshape(dp_count, slice_width, hidden_width), '...  18.4 us
    all_to_all x1, waiting for transfers between devices, on_device(): lax.all_to_all(local_gate.reshape(dp_count, slice_width, hidden_width), '...  18.3 us
    all_to_all x1, blocking collectives, on_device(): lax.all_to_all(send_x, 'expert', split_axis=0, concat_axis=0, tiled=True)  15 us
    all_to_all x1, waiting for transfers between devices, on_device(): lax.all_to_all(local_up.reshape(dp_count, slice_width, hidden_width), 'dp...  12.4 us
    all_to_all x1, waiting for transfers between devices, on_device(): lax.all_to_all(expert_out.reshape(expert_count, capacity, model_width), '...  5.98 us
    dot_general x4, matrix products, dot_last(): lax.dot_general(left, right, (((1,), (1,)), ((), ())), preferred_element_...  5.78 us
  transfers between devices with their start and end apart: 9, of which 7 were waited for; matrix products, arithmetic and copies ran while one was open for 13% of the time, Pallas kernels for 0%

commit v1 on v0

--- a/solution.py
+++ b/solution.py
@@ -4,6 +4,25 @@
 from jax.sharding import PartitionSpec as P
 
 EXPERTS = 128
+
+
+def spread_packet_all(block_here, link_axis, array_dim):
+    w2 = lax.psum(1, link_axis)
+    tmp = lax.axis_index(link_axis)
+    far_arr, block_next, prior = (w2, tmp, block_here.shape[array_dim])
+    nodes = [i * far_arr if it == array_dim else i for it, i in enumerate(block_here.shape)]
+    value_now = jnp.zeros(nodes, block_here.dtype)
+    taken_in = lax.dynamic_update_slice_in_dim(
+        value_now, block_here, block_next * prior, axis=array_dim
+    )
+    for dev_j in tuple(range(1, far_arr)):
+        block_here = lax.ppermute(
+            block_here, link_axis, [(it, (it + 1) % far_arr) for it in range(far_arr)]
+        )
+        taken_in = lax.dynamic_update_slice_in_dim(
+            taken_in, block_here, (block_next - dev_j) % far_arr * prior, axis=array_dim
+        )
+    return taken_in
 
 
 def dot_last(left, right):
@@ -56,7 +75,7 @@
     )
     gate_full, up_full, down_full = (
         lax.all_gather(w_gate, "dp", axis=1, tiled=True),
-        lax.all_gather(w_up, "dp", axis=1, tiled=True),
+        spread_packet_all(w_up, "dp", 1),
         lax.all_gather(w_down, "dp", axis=2, tiled=True),
     )
     gate_full = gate_full[0]

time: 185 us -> 168 us (0.908)
  waiting for transfers between devices: 101 us -> 85.4 us
  blocking collectives: 15 us -> 0 us
  starting transfers between devices: 24 us -> 35.7 us
  local copies, waits for them, and re-layouts: 3.77 us -> 7.21 us
    all_gather x1, waiting for transfers between devices: 19.5 us -> 0.02 us  [on_device(): lax.all_gather(w_down, 'dp', axis=2, tiled=True)]
    all_gather x1 -> x0, waiting for transfers between devices: 19.1 us -> none  [on_device(): lax.all_gather(w_up, 'dp', axis=1, tiled=True)]
    all_to_all x1 -> x0, blocking collectives: 15 us -> none  [on_device(): lax.all_to_all(send_x, 'expert', split_axis=0, concat_axis=0, tiled=True)]
    all_gather x1, waiting for transfers between devices: 0.02 us -> 10.4 us  [on_device(): lax.all_gather(w_gate, 'dp', axis=1, tiled=True)]
    ppermute x0 -> x3, waiting for transfers between devices: none -> 7.46 us  [spread_packet_all(): lax.ppermute(block_here, link_axis, [(it, (it + 1) % far_arr) for it in r...]
    all_to_all x0 -> x1, waiting for transfers between devices: none -> 6.49 us  [on_device(): lax.all_to_all(send_x, 'expert', split_axis=0, concat_axis=0, tiled=True)]
    all_to_all x0 -> x1, starting transfers between devices: none -> 4.89 us  [on_device(): lax.all_to_all(send_x, 'expert', split_axis=0, concat_axis=0, tiled=True)]
    ppermute x0 -> x3, starting transfers between devices: none -> 4.63 us  [spread_packet_all(): lax.ppermute(block_here, link_axis, [(it, (it + 1) % far_arr) for it in r...]
  transfers between devices with their start and end apart: 9 -> 12, of which waited for: 7 -> 9; matrix products, arithmetic and copies ran while one was open for 13% -> 15% of each run, Pallas kernels for 0% -> 0%
where the time goes in v1:
time: 168 us; the launch traced here: 167 us
  waiting for transfers between devices  85.4 us (51%)
  starting transfers between devices  35.7 us (21%)
  matrix products  17 us (10%)
  between operations  14.3 us (9%)
  other arithmetic  7.89 us (5%)
  local copies, waits for them, and re-layouts  7.21 us (4%)
    all_to_all x1, waiting for transfers between devices, on_device(): lax.all_to_all(local_down.reshape(dp_count, slice_width, hidden_width), '...  18.4 us
    all_to_all x1, waiting for transfers between devices, on_device(): lax.all_to_all(local_gate.reshape(dp_count, slice_width, hidden_width), '...  18.3 us
    all_to_all x1, waiting for transfers between devices, on_device(): lax.all_to_all(local_up.reshape(dp_count, slice_width, hidden_width), 'dp...  12.4 us
    all_gather x1, waiting for transfers between devices, on_device(): lax.all_gather(w_gate, 'dp', axis=1, tiled=True)  10.4 us
    ppermute x3, waiting for transfers between devices, spread_packet_all(): lax.ppermute(block_here, link_axis, [(it, (it + 1) % far_arr) for it in r...  7.46 us
    all_to_all x1, waiting for transfers between devices, on_device(): lax.all_to_all(send_x, 'expert', split_axis=0, concat_axis=0, tiled=True)  6.49 us
    all_to_all x1, waiting for transfers between devices, on_device(): lax.all_to_all(expert_out.reshape(expert_count, capacity, model_width), '...  5.98 us
    all_to_all x1, starting transfers between devices, on_device(): lax.all_to_all(send_dy, 'expert', split_axis=0, concat_axis=0, tiled=True)  5.68 us
  transfers between devices with their start and end apart: 12, of which 9 were waited for; matrix products, arithmetic and copies ran while one was open for 15% of the time, Pallas kernels for 0%

profile of v1, /device:TPU:0, one launch (start us, length us, event | category | flops | bytes accessed | tf_op | source)
XLA Modules:
  0.0 167.4 jit_solution(567033461593028954)
XLA Ops:
  12.4 3.8 %collective-permute-done = bf16[1,512,384]{2,1,0:T(8,128)(2,1)} collective-permute-done((bf16[1,512,384]{2,1,0:T(8,128)(2,1)}, bf16[1,512,384]{2,1,0:T(8,128)(2,1)}, u32[]{:S(2)}, u32[]{:S(2)}) %collective-permute-start) | collective-permute-done | bytes 393248 | tf_op jit(solution)/shard_map/ppermute | solution.py:19
  17.1 5.7 %all-to-all-start.2 = ((bf16[4,16,2048]{2,1,0:T(8,128)(2,1)}), bf16[4,16,2048]{2,1,0:T(8,128)(2,1)S(1)}, u32[]{:S(2)}, u32[]{:S(2)}) async-start(bf16[4,16,2048]{2,1,0:T(8,128)(2,1)} %bitcast.13), calls=%async_computation.2 | async-start | bytes 524288 | tf_op jit(solution)/shard_map/all_to_all | solution.py:86
  23.0 3.6 %collective-permute-done.1 = bf16[1,512,384]{2,1,0:T(8,128)(2,1)} collective-permute-done((bf16[1,512,384]{2,1,0:T(8,128)(2,1)}, bf16[1,512,384]{2,1,0:T(8,128)(2,1)}, u32[]{:S(2)}, u32[]{:S(2)}) %collective-permute-start.1) | collective-permute-done | bytes 393248 | tf_op jit(solution)/shard_map/ppermute | solution.py:19
  26.7 4.1 %collective-permute-start.2 = (bf16[1,512,384]{2,1,0:T(8,128)(2,1)}, bf16[1,512,384]{2,1,0:T(8,128)(2,1)S(1)}, u32[]{:S(2)}, u32[]{:S(2)}) collective-permute-start(bf16[1,512,384]{2,1,0:T(8,128)(2,1)} %collective-permute-done.1), channel_id=1, source_target_pairs={{0,1},{1,2},{2,3},{3,0},{4,5},{5,6},{6,7},{7,4},{8,9},{9,10},{10,1... | collective-permute-start | bytes 1179656 | tf_op jit(solution)/shard_map/ppermute | solution.py:19
  32.9 4.9 %all-to-all-start = ((bf16[4,16,2048]{2,1,0:T(8,128)(2,1)}), bf16[4,16,2048]{2,1,0:T(8,128)(2,1)S(1)}, u32[]{:S(2)}, u32[]{:S(2)}) async-start(bf16[4,16,2048]{2,1,0:T(8,128)(2,1)} %bitcast.3), calls=%async_computation | async-start | bytes 524288 | tf_op jit(solution)/shard_map/all_to_all | solution.py:85
  37.9 2.0 %fusion.1 = f32[64,384]{1,0:T(8,128)S(1)} fusion(bf16[64,2048]{1,0:T(8,128)(2,1)S(1)} %bitcast.73, bf16[1,384,2048]{2,1,0:T(8,128)(2,1)} %all-gather.5.cloned.1.call-done), kind=kOutput, calls=%fused_computation.10 | convolution fusion | flops 100663296 | bytes 1933312 | tf_op jit(solution)/shard_map/dot_general | solution.py:29
  39.9 6.5 %all-to-all-done = bf16[4,16,2048]{2,1,0:T(8,128)(2,1)S(1)} async-done(((bf16[4,16,2048]{2,1,0:T(8,128)(2,1)}), bf16[4,16,2048]{2,1,0:T(8,128)(2,1)S(1)}, u32[]{:S(2)}, u32[]{:S(2)}) %all-to-all-start) | async-done | bytes 262176 | tf_op jit(solution)/shard_map/all_to_all | solution.py:85
  46.4 10.4 %all-gather.3.cloned.1.call-done = bf16[1,2048,384]{2,1,0:T(8,128)(2,1)} async-done(((bf16[1,512,384]{2,1,0:T(8,128)(2,1)}), bf16[1,2048,384]{2,1,0:T(8,128)(2,1)}) %all-gather.3.cloned.1.call-update) | async-done | bytes 1572880 | tf_op jit(solution)/shard_map/all_gather | solution.py:77
  61.1 4.6 %all-to-all-start.1 = ((bf16[4,16,2048]{2,1,0:T(8,128)(2,1)}), bf16[4,16,2048]{2,1,0:T(8,128)(2,1)S(1)}, u32[]{:S(2)}, u32[]{:S(2)}) async-start(bf16[4,16,2048]{2,1,0:T(8,128)(2,1)} %bitcast.11), calls=%async_computation.1 | async-start | bytes 524288 | tf_op jit(solution)/shard_map/all_to_all | solution.py:94
  65.7 2.0 %fusion.4 = f32[64,2048]{1,0:T(8,128)S(1)} fusion(bf16[64,384]{1,0:T(8,128)(2,1)S(1)} %get-tuple-element.28, bf16[1,2048,384]{2,1,0:T(8,128)(2,1)} %all-gather.3.cloned.1.call-done), kind=kOutput, calls=%fused_computation.13 | convolution fusion | flops 100663296 | bytes 2146304 | tf_op jit(solution)/shard_map/dot_general | solution.py:29
  69.0 6.0 %all-to-all-done.1 = bf16[4,16,2048]{2,1,0:T(8,128)(2,1)S(1)} async-done(((bf16[4,16,2048]{2,1,0:T(8,128)(2,1)}), bf16[4,16,2048]{2,1,0:T(8,128)(2,1)S(1)}, u32[]{:S(2)}, u32[]{:S(2)}) %all-to-all-start.1) | async-done | bytes 262176 | tf_op jit(solution)/shard_map/all_to_all | solution.py:94
  75.0 3.4 %all-to-all-start.3 = ((bf16[4,16,2048]{2,1,0:T(8,128)(2,1)}), bf16[4,16,2048]{2,1,0:T(8,128)(2,1)S(1)}, u32[]{:S(2)}, u32[]{:S(2)}) async-start(bf16[4,16,2048]{2,1,0:T(8,128)(2,1)} %bitcast.15), calls=%async_computation.3 | async-start | bytes 524288 | tf_op jit(solution)/shard_map/all_to_all | solution.py:101
  78.4 1.8 %convolution_convert_fusion.2 = bf16[2048,384]{1,0:T(8,128)(2,1)} fusion(bf16[64,2048]{1,0:T(8,128)(2,1)S(1)} %bitcast.66, bf16[64,384]{1,0:T(8,128)(2,1)S(1)} %get-tuple-element.28), kind=kOutput, calls=%fused_computation.4 | convolution fusion | flops 101449728 | bytes 1884160 | tf_op jit(solution)/shard_map/sd,sf->df/dot_general | solution.py:121
  80.2 5.1 %all-to-all-done.3 = bf16[4,16,2048]{2,1,0:T(8,128)(2,1)S(1)} async-done(((bf16[4,16,2048]{2,1,0:T(8,128)(2,1)}), bf16[4,16,2048]{2,1,0:T(8,128)(2,1)S(1)}, u32[]{:S(2)}, u32[]{:S(2)}) %all-to-all-start.3) | async-done | bytes 262176 | tf_op jit(solution)/shard_map/all_to_all | solution.py:101
  85.3 3.6 %all-to-all-start.4 = ((bf16[4,512,384]{2,1,0:T(8,128)(2,1)}), bf16[4,512,384]{2,1,0:T(8,128)(2,1)S(1)}, u32[]{:S(2)}, u32[]{:S(2)}) async-start(bf16[4,512,384]{2,1,0:T(8,128)(2,1)} %bitcast.70), calls=%async_computation.4 | async-start | bytes 3145728 | tf_op jit(solution)/shard_map/all_to_all | solution.py:131
  88.9 1.8 %convolution_convert_fusion = bf16[2048,384]{1,0:T(8,128)(2,1)} fusion(bf16[64,2048]{1,0:T(8,128)(2,1)S(1)} %bitcast.74, bf16[64,384]{1,0:T(8,128)(2,1)S(1)} %get-tuple-element.29), kind=kOutput, calls=%fused_computation.2 | convolution fusion | flops 101449728 | bytes 1884160 | tf_op jit(solution)/shard_map/sd,sf->df/dot_general | solution.py:127
  90.7 18.3 %all-to-all-done.4 = bf16[4,512,384]{2,1,0:T(8,128)(2,1)S(1)} async-done(((bf16[4,512,384]{2,1,0:T(8,128)(2,1)}), bf16[4,512,384]{2,1,0:T(8,128)(2,1)S(1)}, u32[]{:S(2)}, u32[]{:S(2)}) %all-to-all-start.4) | async-done | bytes 1572896 | tf_op jit(solution)/shard_map/all_to_all | solution.py:131
  109.0 4.3 %all-to-all-start.6 = ((bf16[4,512,384]{2,1,0:T(8,128)(2,1)}), bf16[4,512,384]{2,1,0:T(8,128)(2,1)}, u32[]{:S(2)}, u32[]{:S(2)}) async-start(bf16[4,512,384]{2,1,0:T(8,128)(2,1)} %bitcast.69), calls=%async_computation.6 | async-start | bytes 3145728 | tf_op jit(solution)/shard_map/all_to_all | solution.py:145
  113.3 1.8 %convolution_convert_fusion.1 = bf16[2048,384]{1,0:T(8,128)(2,1)} fusion(bf16[64,2048]{1,0:T(8,128)(2,1)S(1)} %bitcast.67, bf16[64,384]{1,0:T(8,128)(2,1)S(1)} %get-tuple-element.27), kind=kOutput, calls=%fused_computation.3 | convolution fusion | flops 101449728 | bytes 1884160 | tf_op jit(solution)/shard_map/sd,sf->df/dot_general | solution.py:124
  115.1 18.4 %all-to-all-done.6 = bf16[4,512,384]{2,1,0:T(8,128)(2,1)} async-done(((bf16[4,512,384]{2,1,0:T(8,128)(2,1)}), bf16[4,512,384]{2,1,0:T(8,128)(2,1)}, u32[]{:S(2)}, u32[]{:S(2)}) %all-to-all-start.6) | async-done | bytes 1572896 | tf_op jit(solution)/shard_map/all_to_all | solution.py:145
  133.5 4.5 %all-to-all-start.5 = ((bf16[4,512,384]{2,1,0:T(8,128)(2,1)}), bf16[4,512,384]{2,1,0:T(8,128)(2,1)}, u32[]{:S(2)}, u32[]{:S(2)}) async-start(bf16[4,512,384]{2,1,0:T(8,128)(2,1)} %bitcast.68), calls=%async_computation.5 | async-start | bytes 3145728 | tf_op jit(solution)/shard_map/all_to_all | solution.py:138
  141.9 1.8 %reduce_sum.78 = bf16[512,384]{1,0:T(8,128)(2,1)S(1)} reduce(bf16[4,512,384]{2,1,0:T(8,128)(2,1)} %all-to-all-done.6, bf16[]{:T(256)} %constant.84.clone.1), dimensions={0}, to_apply=%region_9.11 | reduce | flops 589824 | bytes 1966082 | tf_op jit(solution)/shard_map/reduce_sum | solution.py:155
  145.7 12.4 %all-to-all-done.5 = bf16[4,512,384]{2,1,0:T(8,128)(2,1)} async-done(((bf16[4,512,384]{2,1,0:T(8,128)(2,1)}), bf16[4,512,384]{2,1,0:T(8,128)(2,1)}, u32[]{:S(2)}, u32[]{:S(2)}) %all-to-all-start.5) | async-done | bytes 1572896 | tf_op jit(solution)/shard_map/all_to_all | solution.py:138
  158.1 2.5 %reduce_sum.77 = bf16[512,384]{1,0:T(8,128)(2,1)} reduce(bf16[4,512,384]{2,1,0:T(8,128)(2,1)} %all-to-all-done.5, bf16[]{:T(256)} %constant.84.clone.1), dimensions={0}, to_apply=%region_8.10 | reduce | flops 589824 | bytes 1966082 | tf_op jit(solution)/shard_map/reduce_sum | solution.py:154
  (59 shorter events, 20.0 us)
Async XLA Ops:
  7.2 3.5 %copy-start = (bf16[128,2048]{1,0:T(8,128)(2,1)S(1)}, bf16[128,2048]{1,0:T(8,128)(2,1)}, u32[]{:S(2)}) copy-start(bf16[128,2048]{1,0:T(8,128)(2,1)} %param.10) | copy-start | bytes 1572868
  7.2 30.7 %all-gather.5.cloned.1.call-start = ((), (), s32[]{:S(2)}) async-start(), calls=%async_computation.8 | async-start | bytes 1966080 | tf_op jit(solution)/shard_map/all_gather | solution.py:79
  7.9 48.9 %all-gather.3.cloned.1.call-start = ((), (), s32[]{:S(2)}) async-start(), calls=%async_computation.7 | async-start | bytes 1966080 | tf_op jit(solution)/shard_map/all_gather | solution.py:77
  8.0 8.2 %collective-permute-start = (bf16[1,512,384]{2,1,0:T(8,128)(2,1)}, bf16[1,512,384]{2,1,0:T(8,128)(2,1)}, u32[]{:S(2)}, u32[]{:S(2)}) collective-permute-start(bf16[1,512,384]{2,1,0:T(8,128)(2,1)} %param.14), channel_id=1, source_target_pairs={{0,1},{1,2},{2,3},{3,0},{4,5},{5,6},{6,7},{7,4},{8,9},{9,10},{10,1... | collective-permute-start | bytes 1179656 | tf_op jit(solution)/shard_map/ppermute | solution.py:19
  10.1 1.3 copy-start.1
  12.3 10.6 %copy-start.3 = (bf16[1,512,384]{2,1,0:T(8,128)(2,1)S(1)}, bf16[1,512,384]{2,1,0:T(8,128)(2,1)}, u32[]{:S(2)}) copy-start(bf16[1,512,384]{2,1,0:T(8,128)(2,1)} %param.14) | copy-start | bytes 1179652
  16.2 10.5 %collective-permute-start.1 = (bf16[1,512,384]{2,1,0:T(8,128)(2,1)}, bf16[1,512,384]{2,1,0:T(8,128)(2,1)}, u32[]{:S(2)}, u32[]{:S(2)}) collective-permute-start(bf16[1,512,384]{2,1,0:T(8,128)(2,1)} %collective-permute-done), channel_id=1, source_target_pairs={{0,1},{1,2},{2,3},{3,0},{4,5},{5,6},{6,7},{7,4},{8,9},{9,10},{10,1... | collective-permute-start | bytes 1179656 | tf_op jit(solution)/shard_map/ppermute | solution.py:19
  17.1 15.8 %all-to-all-start.2 = ((bf16[4,16,2048]{2,1,0:T(8,128)(2,1)}), bf16[4,16,2048]{2,1,0:T(8,128)(2,1)S(1)}, u32[]{:S(2)}, u32[]{:S(2)}) async-start(bf16[4,16,2048]{2,1,0:T(8,128)(2,1)} %bitcast.13), calls=%async_computation.2 | async-start | bytes 524288 | tf_op jit(solution)/shard_map/all_to_all | solution.py:86
  26.7 11.2 %collective-permute-start.2 = (bf16[1,512,384]{2,1,0:T(8,128)(2,1)}, bf16[1,512,384]{2,1,0:T(8,128)(2,1)S(1)}, u32[]{:S(2)}, u32[]{:S(2)}) collective-permute-start(bf16[1,512,384]{2,1,0:T(8,128)(2,1)} %collective-permute-done.1), channel_id=1, source_target_pairs={{0,1},{1,2},{2,3},{3,0},{4,5},{5,6},{6,7},{7,4},{8,9},{9,10},{10,1... | collective-permute-start | bytes 1179656 | tf_op jit(solution)/shard_map/ppermute | solution.py:19
  32.9 13.5 %all-to-all-start = ((bf16[4,16,2048]{2,1,0:T(8,128)(2,1)}), bf16[4,16,2048]{2,1,0:T(8,128)(2,1)S(1)}, u32[]{:S(2)}, u32[]{:S(2)}) async-start(bf16[4,16,2048]{2,1,0:T(8,128)(2,1)} %bitcast.3), calls=%async_computation | async-start | bytes 524288 | tf_op jit(solution)/shard_map/all_to_all | solution.py:85
  58.6 1.4 copy-start.2
  61.1 13.9 %all-to-all-start.1 = ((bf16[4,16,2048]{2,1,0:T(8,128)(2,1)}), bf16[4,16,2048]{2,1,0:T(8,128)(2,1)S(1)}, u32[]{:S(2)}, u32[]{:S(2)}) async-start(bf16[4,16,2048]{2,1,0:T(8,128)(2,1)} %bitcast.11), calls=%async_computation.1 | async-start | bytes 524288 | tf_op jit(solution)/shard_map/all_to_all | solution.py:94
  75.0 10.3 %all-to-all-start.3 = ((bf16[4,16,2048]{2,1,0:T(8,128)(2,1)}), bf16[4,16,2048]{2,1,0:T(8,128)(2,1)S(1)}, u32[]{:S(2)}, u32[]{:S(2)}) async-start(bf16[4,16,2048]{2,1,0:T(8,128)(2,1)} %bitcast.15), calls=%async_computation.3 | async-start | bytes 524288 | tf_op jit(solution)/shard_map/all_to_all | solution.py:101
  85.3 23.6 %all-to-all-start.4 = ((bf16[4,512,384]{2,1,0:T(8,128)(2,1)}), bf16[4,512,384]{2,1,0:T(8,128)(2,1)S(1)}, u32[]{:S(2)}, u32[]{:S(2)}) async-start(bf16[4,512,384]{2,1,0:T(8,128)(2,1)} %bitcast.70), calls=%async_computation.4 | async-start | bytes 3145728 | tf_op jit(solution)/shard_map/all_to_all | solution.py:131
  109.0 24.5 %all-to-all-start.6 = ((bf16[4,512,384]{2,1,0:T(8,128)(2,1)}), bf16[4,512,384]{2,1,0:T(8,128)(2,1)}, u32[]{:S(2)}, u32[]{:S(2)}) async-start(bf16[4,512,384]{2,1,0:T(8,128)(2,1)} %bitcast.69), calls=%async_computation.6 | async-start | bytes 3145728 | tf_op jit(solution)/shard_map/all_to_all | solution.py:145
  133.5 4.6 %copy-start.4 = (s32[128,8]{0,1:T(8,128)S(1)}, s32[128,8]{0,1:T(8,128)}, u32[]{:S(2)}) copy-start(s32[128,8]{0,1:T(8,128)} %param.11) | copy-start | bytes 12292
  133.5 5.0 %copy-start.5 = (f32[128,8]{0,1:T(8,128)S(1)}, f32[128,8]{0,1:T(8,128)}, u32[]{:S(2)}) copy-start(f32[128,8]{0,1:T(8,128)} %param.12) | copy-start | bytes 12292
  133.5 24.6 %all-to-all-start.5 = ((bf16[4,512,384]{2,1,0:T(8,128)(2,1)}), bf16[4,512,384]{2,1,0:T(8,128)(2,1)}, u32[]{:S(2)}, u32[]{:S(2)}) async-start(bf16[4,512,384]{2,1,0:T(8,128)(2,1)} %bitcast.68), calls=%async_computation.5 | async-start | bytes 3145728 | tf_op jit(solution)/shard_map/all_to_all | solution.py:138
Sparse Core Ops, SparseCore 0:
  9.6 24.9 all-gather.4
  36.2 20.6 all-gather.2
